TPU v7x, 128 devices: a whole 4x4x4 slice. The times are simulated.
128 devices in a mesh: arc: 16 (over x, z), vec: 8 (over y, core).
Axes of the slice: x: 4, y: 4, z: 4, core: 2. Of those that a mesh axis runs over, the one named last changes fastest.
Arguments:
- right_side: float32 [640, 128, 128], P(('arc', 'vec')), may hold values from -6 to 6
- prior_diag: float32 [640, 128], P(('arc', 'vec')), may hold values from 0.5 to 4
- inv_factor: bfloat16 [2048, 256, 256], P(('arc', 'vec'))
- coupling_panel: bfloat16 [2048, 256, 1024], P(('arc', 'vec')), may hold values from -0.09375 to 0.09375
- coupling_owner: int32 [2048, 8], replicated, may hold values from 0 to 127, all different within a row; in each aligned block of 16 rows (0 to 15, 16 to 31, ...) at most 2 rows name the same one
- coupling_block: int32 [2048, 8], replicated, may hold values from 0 to 4
Outputs:
- solution_field: float32 [640, 128, 128], P(('arc', 'vec'))
- residual: float32 [640, 128, 128], P(('arc', 'vec'))
Inputs may be any that keep to these rules, and one draw needn't show every extreme that they name: `coupling_owner`: the 8 holders named for one arc are different. Among the 16 arcs of one device (aligned blocks of rows) no holder is named more than 2 times; some holder is named exactly 2 times.
All inputs are finite; a program needn't handle non-finite values.
Results may differ from a plain program's by a relative error of at most 0.006.
The roundings to bfloat16 on the way count: a program that leaves them out, or rounds other values in their place, can miss the bound.
Values may be sent and summed in bfloat16 or wider, within the bound.
A program may use at most 128 MiB of HBM per device.

v0:
```python
import jax
import jax.numpy as jnp
from jax import lax
from jax.sharding import PartitionSpec as P

ITERS = 2


def inner_gram(left, right):
    return jnp.einsum("grc,grd->cd", left, right, precision=lax.Precision.HIGHEST)


def combine_cols(field, weights):
    return jnp.einsum("grc,cd->grd", field, weights, precision=lax.Precision.HIGHEST)


def trade_out(buffer):
    return lax.all_to_all(buffer, ("arc", "vec"), split_axis=0, concat_axis=0, tiled=True)


def trade_back(buffer):
    return lax.all_to_all(buffer, ("arc", "vec"), split_axis=0, concat_axis=0, tiled=True)


def per_device(right_side, prior_diag, inv_factor, coupling_panel, coupling_owner, coupling_block):
    device_count = lax.axis_size(("arc", "vec"))
    my_index = lax.axis_index(("arc", "vec"))
    arcs_here = coupling_panel.shape[0]
    links = coupling_owner.shape[1]
    blocks_here = right_side.shape[0]
    block_rows = right_side.shape[1]
    rhs_count = right_side.shape[2]
    entries = arcs_here * links
    slot_count = (entries + device_count - 1) // device_count + 1
    owner_all = coupling_owner.reshape(device_count, entries)
    block_all = coupling_block.reshape(device_count, entries)
    position = jnp.arange(entries, dtype=jnp.int32)
    earlier = (owner_all[:, :, None] == owner_all[:, None, :]) & (
        position[None, None, :] < position[None, :, None]
    )
    rank_all = jnp.sum(earlier.astype(jnp.int32), axis=2)
    owner_mine = lax.dynamic_index_in_dim(owner_all, my_index, 0, keepdims=False)
    rank_mine = lax.dynamic_index_in_dim(rank_all, my_index, 0, keepdims=False)
    slot_mine = owner_mine * slot_count + rank_mine
    slot_ids = jnp.arange(slot_count, dtype=jnp.int32)
    matches = (owner_all[:, None, :] == my_index) & (
        rank_all[:, None, :] == slot_ids[None, :, None]
    )
    filled = jnp.any(matches, axis=2).reshape(-1)
    source_block = jnp.sum(jnp.where(matches, block_all[:, None, :], 0), axis=2).reshape(-1)
    block_ids = jnp.arange(blocks_here, dtype=jnp.int32)
    selector = ((source_block[:, None] == block_ids[None, :]) & filled[:, None]).astype(
        jnp.bfloat16
    )
    solution_field = jnp.zeros_like(right_side)
    residual = right_side
    direction = right_side
    res_gram = lax.psum(inner_gram(residual, residual), ("arc", "vec"))
    for sweep_index in range(ITERS):
        local_rounded = direction.astype(jnp.bfloat16)
        outgoing = jnp.where(
            filled[:, None, None], local_rounded[source_block], jnp.zeros((), jnp.bfloat16)
        )
        arrived = trade_out(outgoing)
        fetched = arrived[slot_mine].reshape(arcs_here, links * block_rows, rhs_count)
        coupled = jnp.einsum(
            "apk,akc->apc", coupling_panel, fetched, preferred_element_type=jnp.float32
        ).astype(jnp.bfloat16)
        whitened = jnp.einsum(
            "apq,aqc->apc", inv_factor, coupled, preferred_element_type=jnp.float32
        ).astype(jnp.bfloat16)
        smoothed = jnp.einsum(
            "aqp,aqc->apc", inv_factor, whitened, preferred_element_type=jnp.float32
        ).astype(jnp.bfloat16)
        projected = jnp.einsum(
            "apk,apc->akc", coupling_panel, smoothed, preferred_element_type=jnp.float32
        ).astype(jnp.bfloat16)
        projected = projected.reshape(entries, block_rows, rhs_count)
        returning = (
            jnp.zeros((device_count * slot_count, block_rows, rhs_count), jnp.bfloat16)
            .at[slot_mine]
            .set(projected)
        )
        came_back = trade_back(returning)
        summed = jnp.einsum("sb,src->brc", selector, came_back, preferred_element_type=jnp.float32)
        image_vec = prior_diag[:, :, None] * direction + summed
        curv_gram = lax.psum(inner_gram(direction, image_vec), ("arc", "vec"))
        factor_low = jnp.linalg.cholesky(curv_gram)
        step_mat = jax.scipy.linalg.cho_solve((factor_low, True), res_gram)
        solution_field = solution_field + combine_cols(direction, step_mat)
        residual = residual - combine_cols(image_vec, step_mat)
        if sweep_index + 1 < ITERS:
            new_gram = lax.psum(inner_gram(residual, residual), ("arc", "vec"))
            beta_mat = jax.scipy.linalg.cho_solve((jnp.linalg.cholesky(res_gram), True), new_gram)
            direction = residual + combine_cols(direction, beta_mat)
            res_gram = new_gram
    return (solution_field, residual)


def solution(mesh):
    in_specs = (
        P(("arc", "vec"), None, None),
        P(("arc", "vec"), None),
        P(("arc", "vec"), None, None),
        P(("arc", "vec"), None, None),
        P(),
        P(),
    )
    out_specs = (P(("arc", "vec"), None, None), P(("arc", "vec"), None, None))
    return jax.shard_map(
        per_device, mesh=mesh, in_specs=in_specs, out_specs=out_specs, check_vma=False
    )
```

profile of v0, /device:TPU:1, one launch (start us, length us, event | category | flops | bytes accessed | tf_op | source)
XLA Modules:
  0.0 1105.9 jit_solution(6747091864298645977)
XLA Ops:
  7.2 1.3 copy.134
  8.5 0.5 broadcast_in_dim_reshape.2
  9.1 5.1 convert_reduce_fusion
  14.6 1.2 copy.135
  15.8 0.5 broadcast_in_dim.29
  16.7 1.0 convert_element_type.47
  17.7 8.3 gather_fusion
  26.0 7.2 broadcast_select_fusion.1
  33.3 12.3 %all-to-all-start = ((bf16[256,128,128]{2,1,0:T(8,128)(2,1)}), bf16[256,128,128]{2,1,0:T(8,128)(2,1)}, u32[]{:S(2)}, u32[]{:S(2)}) async-start(bf16[256,128,128]{2,1,0:T(8,128)(2,1)} %broadcast_select_fusion.1), calls=%async_computation | async-start | bytes 16777216 | tf_op jit(solution)/shard_map/all_to_all | solution.py:18
  45.7 106.4 %all-to-all-done = bf16[256,128,128]{2,1,0:T(8,128)(2,1)} async-done(((bf16[256,128,128]{2,1,0:T(8,128)(2,1)}), bf16[256,128,128]{2,1,0:T(8,128)(2,1)}, u32[]{:S(2)}, u32[]{:S(2)}) %all-to-all-start) | async-done | bytes 8388640 | tf_op jit(solution)/shard_map/all_to_all | solution.py:18
  152.0 6.4 gather_fusion.1
  158.5 8.2 convolution_convert_fusion.4
  166.7 6.9 convert_bitcast_fusion.1
  173.6 6.4 copy.140
  180.0 5.3 broadcast.116.clone
  185.3 19.4 %scatter_fusion = bf16[256,128,128]{2,1,0:T(8,128)(2,1)} fusion(bf16[256,128,128]{2,1,0:T(8,128)(2,1)} %broadcast.116.clone, s32[128]{0:T(128)S(1)} %fusion.34, bf16[128,128,128]{2,1,0:T(8,128)(2,1)} %bitcast.106), kind=kCustom, calls=%fused_computation.4 | custom fusion | bytes 12583424 | tf_op jit(solution)/shard_map/scatter | solution.py:82
  204.7 6.8 all-to-all-start.1
  211.8 1.3 convolution_bitcast_fusion.7
  213.2 104.7 %all-to-all-done.1 = bf16[256,128,128]{2,1,0:T(8,128)(2,1)} async-done(((bf16[256,128,128]{2,1,0:T(8,128)(2,1)}), bf16[256,128,128]{2,1,0:T(8,128)(2,1)}, u32[]{:S(2)}, u32[]{:S(2)}) %all-to-all-start.1) | async-done | bytes 8388640 | tf_op jit(solution)/shard_map/all_to_all | solution.py:22
  317.9 7.8 fusion.2
  325.7 1.4 convolution_bitcast_fusion.8
  327.5 139.7 %all-reduce.9.cloned.1.call-done = (f32[128,128]{0,1:T(8,128)}, f32[128,128]{0,1:T(8,128)}) async-done(((f32[128,128]{0,1:T(8,128)}, f32[128,128]{0,1:T(8,128)}), (f32[128,128]{0,1:T(8,128)}, f32[128,128]{0,1:T(8,128)})) %all-reduce.9.cloned.1.call-update) | async-done | bytes 131088 | tf_op jit(solution)/shard_map/psum | solution.py:58
  467.2 0.9 copy.148
  468.1 0.9 copy.144
  469.1 0.9 fusion.21
  470.0 11.7 %cholesky.70 = f32[128,128]{1,0:T(8,128)S(1)} custom-call(f32[128,128]{1,0:T(8,128)S(1)} %get-tuple-element.18), custom_call_target="Cholesky" | custom-call | tf_op jit(solution)/shard_map/jit(cholesky)/cholesky | solution.py:94
  481.7 0.7 compare_reduce_fusion.1
  482.4 11.7 %cholesky.59 = f32[128,128]{1,0:T(8,128)S(1)} custom-call(f32[128,128]{1,0:T(8,128)S(1)} %get-tuple-element.19), custom_call_target="Cholesky" | custom-call | tf_op jit(solution)/shard_map/jit(cholesky)/cholesky | solution.py:88
  494.1 0.6 compare_reduce_fusion.2
  494.8 0.7 fusion.11
  495.5 9.8 custom-call.9
  505.3 1.1 fusion.23
  506.6 0.5 convolution_subtract_fusion.1
  507.1 1.3 convolution_bitcast_fusion.5
  508.4 10.2 all-reduce.7.cloned.1.call-start
  518.7 1.5 fusion.12
  520.1 9.8 custom-call.10
  530.0 114.2 %all-reduce.5.cloned.1.call-done = f32[128,128]{1,0:T(8,128)} async-done(((f32[128,128]{1,0:T(8,128)}), f32[128,128]{1,0:T(8,128)}) %all-reduce.5.cloned.1.call-update) | async-done | bytes 65552 | tf_op jit(solution)/shard_map/psum | solution.py:93
  644.2 1.1 fusion.19
  645.6 0.4 fusion.35
  646.0 8.3 gather_fusion.2
  654.4 7.2 broadcast_select_fusion
  661.6 103.7 %all_to_all.20 = bf16[256,128,128]{2,1,0:T(8,128)(2,1)} all-to-all(bf16[256,128,128]{2,1,0:T(8,128)(2,1)} %broadcast_select_fusion), channel_id=1, replica_groups=mesh['arc'=16,'vec'=8] {'arc','vec'}, dimensions={0} | all-to-all | bytes 16777216 | tf_op jit(solution)/shard_map/all_to_all | solution.py:18
  765.3 6.4 gather_fusion.3
  771.8 9.2 convolution_convert_fusion.1
  781.0 7.2 convert_bitcast_fusion
  788.2 6.4 copy.153
  794.6 5.3 broadcast.116
  799.9 19.4 %scatter_fusion.1 = bf16[256,128,128]{2,1,0:T(8,128)(2,1)} fusion(bf16[256,128,128]{2,1,0:T(8,128)(2,1)} %broadcast.116, s32[128]{0:T(128)S(1)} %fusion.34, bf16[128,128,128]{2,1,0:T(8,128)(2,1)} %bitcast.105), kind=kCustom, calls=%fused_computation.5 | custom fusion | bytes 12583424 | tf_op jit(solution)/shard_map/scatter | solution.py:82
  819.3 106.0 %all_to_all.21 = bf16[256,128,128]{2,1,0:T(8,128)(2,1)S(1)} all-to-all(bf16[256,128,128]{2,1,0:T(8,128)(2,1)} %scatter_fusion.1), channel_id=1, replica_groups=mesh['arc'=16,'vec'=8] {'arc','vec'}, dimensions={0} | all-to-all | bytes 16777216 | tf_op jit(solution)/shard_map/all_to_all | solution.py:22
  925.3 4.5 fusion
  929.7 0.8 copy-done.2
  930.5 1.5 convolution_bitcast_fusion.3
  932.0 1.2 convolution_bitcast_fusion.1
  933.2 136.1 %all-reduce.7.cloned.1.call-done = f32[128,128]{0,1:T(8,128)} async-done(((f32[128,128]{0,1:T(8,128)}), f32[128,128]{0,1:T(8,128)}) %all-reduce.7.cloned.1.call-update) | async-done | bytes 65552 | tf_op jit(solution)/shard_map/psum | solution.py:87
  1069.3 0.9 copy.158
  1070.3 0.9 fusion.17
  1071.1 11.7 %cholesky.81 = f32[128,128]{1,0:T(8,128)S(1)} custom-call(f32[128,128]{1,0:T(8,128)S(1)} %fusion.17), custom_call_target="Cholesky" | custom-call | tf_op jit(solution)/shard_map/jit(cholesky)/cholesky | solution.py:88
  1082.9 0.6 compare_reduce_fusion
  1083.5 0.7 fusion.13
  1084.2 9.8 custom-call.11
  1094.5 2.2 convolution_subtract_fusion
  1096.7 1.5 convolution_add_fusion
  1098.2 0.9 copy.160
  (36 shorter events, 2.7 us)
Async XLA Ops:
  7.2 151.3 %copy-start = (bf16[16,256,256]{2,1,0:T(8,128)(2,1)S(1)}, bf16[16,256,256]{2,1,0:T(8,128)(2,1)}, u32[]{:S(2)}) copy-start(bf16[16,256,256]{2,1,0:T(8,128)(2,1)} %param.11) | copy-start | bytes 6291460
  33.3 118.8 %all-to-all-start = ((bf16[256,128,128]{2,1,0:T(8,128)(2,1)}), bf16[256,128,128]{2,1,0:T(8,128)(2,1)}, u32[]{:S(2)}, u32[]{:S(2)}) async-start(bf16[256,128,128]{2,1,0:T(8,128)(2,1)} %broadcast_select_fusion.1), calls=%async_computation | async-start | bytes 16777216 | tf_op jit(solution)/shard_map/all_to_all | solution.py:18
  204.7 7.2 copy-start.1
  204.7 113.2 %all-to-all-start.1 = ((bf16[256,128,128]{2,1,0:T(8,128)(2,1)}), bf16[256,128,128]{2,1,0:T(8,128)(2,1)}, u32[]{:S(2)}, u32[]{:S(2)}) async-start(bf16[256,128,128]{2,1,0:T(8,128)(2,1)} %scatter_fusion), calls=%async_computation.1 | async-start | bytes 16777216 | tf_op jit(solution)/shard_map/all_to_all | solution.py:22
  211.4 114.3 %copy-start.5 = (f32[5,128]{1,0:T(8,128)S(1)}, f32[5,128]{1,0:T(8,128)}, u32[]{:S(2)}) copy-start(f32[5,128]{1,0:T(8,128)} %param.10) | copy-start | bytes 7684
  211.4 255.8 %all-reduce.9.cloned.1.call-start = ((), (), s32[]{:S(2)}) async-start(), calls=%async_computation.6 | async-start | bytes 262144 | tf_op jit(solution)/shard_map/psum | solution.py:58
  327.2 317.0 %all-reduce.5.cloned.1.call-start = ((), (), s32[]{:S(2)}) async-start(), calls=%async_computation.4 | async-start | bytes 131072 | tf_op jit(solution)/shard_map/psum | solution.py:93
  481.7 13.1 %copy-start.4 = (f32[128,128]{1,0:T(8,128)}, f32[128,128]{1,0:T(8,128)S(1)}, u32[]{:S(2)}) copy-start(f32[128,128]{1,0:T(8,128)S(1)} %cholesky.70) | copy-start | bytes 196612
  508.4 560.9 %all-reduce.7.cloned.1.call-start = ((), (), s32[]{:S(2)}) async-start(), calls=%async_computation.5 | async-start | bytes 131072 | tf_op jit(solution)/shard_map/psum | solution.py:87
  925.3 168.7 %copy-start.3 = (f32[128,128]{1,0:T(8,128)S(1)}, f32[128,128]{1,0:T(8,128)}, u32[]{:S(2)}) copy-start(f32[128,128]{1,0:T(8,128)} %all-reduce.5.cloned.1.call-done) | copy-start | bytes 196612
  929.7 0.8 copy-start.2
Sparse Core Ops, SparseCore 0:
  327.3 139.8 all-reduce.8
  508.6 135.5 all-reduce.4
  932.1 137.1 all-reduce.6
where the time goes:
time: 1110 us
  waiting for transfers between devices  601 us (54%)
  blocking collectives  210 us (19%)
  local copies, waits for them, and re-layouts  100 us (9%)
  other arithmetic  92 us (8%)
  matrix products  58.4 us (5%)
  starting transfers between devices  29.9 us (3%)
  between operations  14.3 us (1%)
    psum x1, waiting for transfers between devices, per_device(): res_gram = lax.psum(inner_gram(residual, residual), ('arc', 'vec'))  140 us
    psum x1, waiting for transfers between devices, per_device(): curv_gram = lax.psum(inner_gram(direction, image_vec), ('arc', 'vec'))  136 us
    psum x1, waiting for transfers between devices, per_device(): new_gram = lax.psum(inner_gram(residual, residual), ('arc', 'vec'))  114 us
    all_to_all x1, waiting for transfers between devices, trade_out(): lax.all_to_all(buffer, ('arc', 'vec'), split_axis=0, concat_axis=0, tiled...  106 us
    all_to_all x1, blocking collectives, trade_back(): lax.all_to_all(buffer, ('arc', 'vec'), split_axis=0, concat_axis=0, tiled...  106 us
    all_to_all x1, waiting for transfers between devices, trade_back(): lax.all_to_all(buffer, ('arc', 'vec'), split_axis=0, concat_axis=0, tiled...  105 us
    all_to_all x1, blocking collectives, trade_out(): lax.all_to_all(buffer, ('arc', 'vec'), split_axis=0, concat_axis=0, tiled...  104 us
    scatter x2, local copies, waits for them, and re-layouts, per_device(): returning = jnp.zeros((device_count * slot_count, block_rows, rhs_count),...  38.7 us
  transfers between devices with their start and end apart: 5, of which 5 were waited for; matrix products, arithmetic and copies ran while one was open for 1% of the time, Pallas kernels for 0%

commit v1 on v0

--- a/solution.py
+++ b/solution.py
@@ -55,7 +55,7 @@
     solution_field = jnp.zeros_like(right_side)
     residual = right_side
     direction = right_side
-    res_gram = lax.psum(inner_gram(residual, residual), ("arc", "vec"))
+    res_gram = lax.psum(lax.psum(inner_gram(residual, residual), "vec"), "arc")
     for sweep_index in range(ITERS):
         local_rounded = direction.astype(jnp.bfloat16)
         outgoing = jnp.where(

time: 1110 us -> 1200 us (1.081)
  waiting for transfers between devices: 601 us -> 694 us
    psum x1 -> x2, waiting for transfers between devices: 136 us -> 273 us  [per_device(): curv_gram = lax.psum(inner_gram(direction, image_vec), ('arc', 'vec'))]
    all_to_all x1, waiting for transfers between devices: 105 us -> 0.01 us  [trade_back(): lax.all_to_all(buffer, ('arc', 'vec'), split_axis=0, concat_axis=0, tiled...]
    psum x1 -> x2, waiting for transfers between devices: 140 us -> 191 us  [per_device(): res_gram = lax.psum(lax.psum(inner_gram(residual, residual), 'vec'), 'arc')]
  transfers between devices with their start and end apart: 5 -> 7, of which waited for: 5 -> 6; matrix products, arithmetic and copies ran while one was open for 1% -> 2% of each run, Pallas kernels for 0% -> 0%
where the time goes in v1:
time: 1200 us; the launch traced here: 1190 us
  waiting for transfers between devices  694 us (58%)
  blocking collectives  211 us (18%)
  local copies, waits for them, and re-layouts  100 us (8%)
  other arithmetic  92.8 us (8%)
  matrix products  57.6 us (5%)
  starting transfers between devices  20.3 us (2%)
  between operations  16.2 us (1%)
    psum x2, waiting for transfers between devices, per_device(): curv_gram = lax.psum(inner_gram(direction, image_vec), ('arc', 'vec'))  273 us
    psum x2, waiting for transfers between devices, per_device(): res_gram = lax.psum(lax.psum(inner_gram(residual, residual), 'vec'), 'arc')  191 us
    psum x1, waiting for transfers between devices, per_device(): new_gram = lax.psum(inner_gram(residual, residual), ('arc', 'vec'))  123 us
    all_to_all x1, blocking collectives, trade_back(): lax.all_to_all(buffer, ('arc', 'vec'), split_axis=0, concat_axis=0, tiled...  107 us
    all_to_all x1, waiting for transfers between devices, trade_out(): lax.all_to_all(buffer, ('arc', 'vec'), split_axis=0, concat_axis=0, tiled...  106 us
    all_to_all x1, blocking collectives, trade_out(): lax.all_to_all(buffer, ('arc', 'vec'), split_axis=0, concat_axis=0, tiled...  104 us
    scatter x2, local copies, waits for them, and re-layouts, per_device(): returning = jnp.zeros((device_count * slot_count, block_rows, rhs_count),...  38.6 us
    another operation x6, other arithmetic, per_device(): factor_low = jnp.linalg.cholesky(curv_gram)  24.8 us
  transfers between devices with their start and end apart: 7, of which 6 were waited for; matrix products, arithmetic and copies ran while one was open for 2% of the time, Pallas kernels for 0%

profile of v1, /device:TPU:1, one launch (start us, length us, event | category | flops | bytes accessed | tf_op | source)
XLA Modules:
  0.0 1191.8 jit_solution(5083724130027614488)
XLA Ops:
  8.0 1.3 copy.134
  9.4 0.5 broadcast_in_dim_reshape.2
  9.9 5.1 convert_reduce_fusion
  15.4 1.2 copy.135
  16.6 0.5 broadcast_in_dim.29
  17.5 1.0 convert_element_type.47
  18.5 8.3 gather_fusion
  26.9 7.2 broadcast_select_fusion.1
  34.1 12.3 %all-to-all-start = ((bf16[256,128,128]{2,1,0:T(8,128)(2,1)}), bf16[256,128,128]{2,1,0:T(8,128)(2,1)}, u32[]{:S(2)}, u32[]{:S(2)}) async-start(bf16[256,128,128]{2,1,0:T(8,128)(2,1)} %broadcast_select_fusion.1), calls=%async_computation | async-start | bytes 16777216 | tf_op jit(solution)/shard_map/all_to_all | solution.py:18
  46.5 106.4 %all-to-all-done = bf16[256,128,128]{2,1,0:T(8,128)(2,1)} async-done(((bf16[256,128,128]{2,1,0:T(8,128)(2,1)}), bf16[256,128,128]{2,1,0:T(8,128)(2,1)}, u32[]{:S(2)}, u32[]{:S(2)}) %all-to-all-start) | async-done | bytes 8388640 | tf_op jit(solution)/shard_map/all_to_all | solution.py:18
  152.9 6.4 gather_fusion.1
  159.3 8.2 convolution_convert_fusion.4
  167.5 6.9 convert_bitcast_fusion.1
  174.5 6.4 copy.140
  180.9 5.3 broadcast.116.clone
  186.2 19.3 %scatter_fusion = bf16[256,128,128]{2,1,0:T(8,128)(2,1)} fusion(bf16[256,128,128]{2,1,0:T(8,128)(2,1)} %broadcast.116.clone, s32[128]{0:T(128)S(1)} %fusion.34, bf16[128,128,128]{2,1,0:T(8,128)(2,1)} %bitcast.106), kind=kCustom, calls=%fused_computation.4 | custom fusion | bytes 12583424 | tf_op jit(solution)/shard_map/scatter | solution.py:82
  205.5 6.8 all-to-all-start.1
  212.4 1.3 convolution_bitcast_fusion.7
  213.8 108.0 %all-reduce.8.cloned.1.call-done = f32[128,128]{0,1:T(8,128)} async-done(((f32[128,128]{0,1:T(8,128)}), f32[128,128]{0,1:T(8,128)}) %all-reduce.8.cloned.1.call-update) | async-done | bytes 65552 | tf_op jit(solution)/shard_map/psum | solution.py:58
  322.2 83.4 %all-reduce.10.cloned.1.call-done = f32[128,128]{0,1:T(8,128)} async-done(((f32[128,128]{0,1:T(8,128)}), f32[128,128]{0,1:T(8,128)}) %all-reduce.10.cloned.1.call-update) | async-done | bytes 65552 | tf_op jit(solution)/shard_map/psum | solution.py:58
  405.6 1.0 copy.148
  406.6 0.9 fusion.21
  407.5 11.7 cholesky.70
  419.2 7.8 fusion.2
  427.1 1.4 convolution_bitcast_fusion.8
  428.8 0.7 compare_reduce_fusion.1
  429.5 137.4 %all-reduce.6.cloned.1.call-done = f32[128,128]{0,1:T(8,128)} async-done(((f32[128,128]{0,1:T(8,128)}), f32[128,128]{0,1:T(8,128)}) %all-reduce.6.cloned.1.call-update) | async-done | bytes 65552 | tf_op jit(solution)/shard_map/psum | solution.py:87
  566.9 0.9 copy.144
  567.8 0.9 fusion.25
  568.7 11.7 cholesky.59
  580.4 0.6 compare_reduce_fusion.2
  581.1 0.7 fusion.11
  581.7 9.8 custom-call.9
  592.1 0.5 convolution_subtract_fusion.1
  592.5 1.3 convolution_bitcast_fusion.5
  593.9 0.5 all-reduce.14.cloned.1.call-start
  594.4 1.5 fusion.12
  595.9 9.8 custom-call.10
  605.7 122.7 %all-reduce.12.cloned.1.call-done = f32[128,128]{1,0:T(8,128)} async-done(((f32[128,128]{1,0:T(8,128)}), f32[128,128]{1,0:T(8,128)}) %all-reduce.12.cloned.1.call-update) | async-done | bytes 65552 | tf_op jit(solution)/shard_map/psum | solution.py:93
  728.4 1.1 fusion.19
  730.3 8.3 gather_fusion.2
  738.6 7.2 broadcast_select_fusion
  745.9 103.9 %all_to_all.20 = bf16[256,128,128]{2,1,0:T(8,128)(2,1)} all-to-all(bf16[256,128,128]{2,1,0:T(8,128)(2,1)} %broadcast_select_fusion), channel_id=1, replica_groups=mesh['arc'=16,'vec'=8] {'arc','vec'}, dimensions={0} | all-to-all | bytes 16777216 | tf_op jit(solution)/shard_map/all_to_all | solution.py:18
  849.7 6.4 gather_fusion.3
  856.2 9.2 convolution_convert_fusion.1
  865.4 7.2 convert_bitcast_fusion
  872.6 6.4 copy.153
  879.0 5.3 broadcast.116
  884.3 19.4 %scatter_fusion.1 = bf16[256,128,128]{2,1,0:T(8,128)(2,1)} fusion(bf16[256,128,128]{2,1,0:T(8,128)(2,1)} %broadcast.116, s32[128]{0:T(128)S(1)} %fusion.34, bf16[128,128,128]{2,1,0:T(8,128)(2,1)} %bitcast.105), kind=kCustom, calls=%fused_computation.5 | custom fusion | bytes 12583424 | tf_op jit(solution)/shard_map/scatter | solution.py:82
  903.7 106.9 %all_to_all.21 = bf16[256,128,128]{2,1,0:T(8,128)(2,1)S(1)} all-to-all(bf16[256,128,128]{2,1,0:T(8,128)(2,1)} %scatter_fusion.1), channel_id=1, replica_groups=mesh['arc'=16,'vec'=8] {'arc','vec'}, dimensions={0} | all-to-all | bytes 16777216 | tf_op jit(solution)/shard_map/all_to_all | solution.py:22
  1010.6 4.5 fusion
  1015.0 0.8 copy-done.2
  1015.8 1.5 convolution_bitcast_fusion.3
  1017.3 1.2 convolution_bitcast_fusion.1
  1018.5 135.7 %all-reduce.14.cloned.1.call-done = f32[128,128]{0,1:T(8,128)} async-done(((f32[128,128]{0,1:T(8,128)}), f32[128,128]{0,1:T(8,128)}) %all-reduce.14.cloned.1.call-update) | async-done | bytes 65552 | tf_op jit(solution)/shard_map/psum | solution.py:87
  1154.2 0.9 copy.158
  1155.1 0.9 fusion.17
  1156.0 11.7 cholesky.81
  1167.7 0.6 compare_reduce_fusion
  1168.3 0.7 fusion.13
  1169.0 9.8 custom-call.11
  1179.3 2.2 convolution_subtract_fusion
  1181.6 1.5 convolution_add_fusion
  1183.0 0.9 copy.160
  (45 shorter events, 3.5 us)
Async XLA Ops:
  8.0 151.3 %copy-start = (bf16[16,256,256]{2,1,0:T(8,128)(2,1)S(1)}, bf16[16,256,256]{2,1,0:T(8,128)(2,1)}, u32[]{:S(2)}) copy-start(bf16[16,256,256]{2,1,0:T(8,128)(2,1)} %param.11) | copy-start | bytes 6291460
  34.1 118.8 %all-to-all-start = ((bf16[256,128,128]{2,1,0:T(8,128)(2,1)}), bf16[256,128,128]{2,1,0:T(8,128)(2,1)}, u32[]{:S(2)}, u32[]{:S(2)}) async-start(bf16[256,128,128]{2,1,0:T(8,128)(2,1)} %broadcast_select_fusion.1), calls=%async_computation | async-start | bytes 16777216 | tf_op jit(solution)/shard_map/all_to_all | solution.py:18
  205.5 6.9 copy-start.1
  205.5 213.7 %all-to-all-start.1 = ((bf16[256,128,128]{2,1,0:T(8,128)(2,1)}), bf16[256,128,128]{2,1,0:T(8,128)(2,1)}, u32[]{:S(2)}, u32[]{:S(2)}) async-start(bf16[256,128,128]{2,1,0:T(8,128)(2,1)} %scatter_fusion), calls=%async_computation.1 | async-start | bytes 16777216 | tf_op jit(solution)/shard_map/all_to_all | solution.py:22
  212.3 214.8 %copy-start.6 = (f32[5,128]{1,0:T(8,128)S(1)}, f32[5,128]{1,0:T(8,128)}, u32[]{:S(2)}) copy-start(f32[5,128]{1,0:T(8,128)} %param.10) | copy-start | bytes 7684
  212.3 109.5 %all-reduce.8.cloned.1.call-start = ((), (), s32[]{:S(2)}) async-start(), calls=%async_computation.5 | async-start | bytes 131072 | tf_op jit(solution)/shard_map/psum | solution.py:58
  213.7 191.9 %all-reduce.10.cloned.1.call-start = ((), (), s32[]{:S(2)}) async-start(), calls=%async_computation.6 | async-start | bytes 131072 | tf_op jit(solution)/shard_map/psum | solution.py:58
  321.8 245.1 %all-reduce.6.cloned.1.call-start = ((), (), s32[]{:S(2)}) async-start(), calls=%async_computation.4 | async-start | bytes 131072 | tf_op jit(solution)/shard_map/psum | solution.py:87
  405.6 186.0 %copy-start.3 = (f32[128,128]{0,1:T(8,128)S(1)}, f32[128,128]{0,1:T(8,128)}, u32[]{:S(2)}) copy-start(f32[128,128]{0,1:T(8,128)} %all-reduce.10.cloned.1.call-done) | copy-start | bytes 196612
  419.2 10.3 copy-start.5
  428.5 299.9 %all-reduce.12.cloned.1.call-start = ((), (), s32[]{:S(2)}) async-start(), calls=%async_computation.7 | async-start | bytes 131072 | tf_op jit(solution)/shard_map/psum | solution.py:93
  593.9 560.3 %all-reduce.14.cloned.1.call-start = ((), (), s32[]{:S(2)}) async-start(), calls=%async_computation.8 | async-start | bytes 131072 | tf_op jit(solution)/shard_map/psum | solution.py:87
  1010.6 168.3 %copy-start.4 = (f32[128,128]{1,0:T(8,128)S(1)}, f32[128,128]{1,0:T(8,128)}, u32[]{:S(2)}) copy-start(f32[128,128]{1,0:T(8,128)} %all-reduce.12.cloned.1.call-done) | copy-start | bytes 196612
  1015.0 0.8 copy-start.2
Sparse Core Ops, SparseCore 0:
  216.0 105.7 all-reduce.7
  325.3 80.2 all-reduce.9
Sparse Core Ops, SparseCore 1:
  428.6 138.2 all-reduce.5
  594.0 134.4 all-reduce.11
  1017.4 136.7 all-reduce.13
